TPU v7x, 256 devices: a whole 4x4x8 slice. The times are simulated.
256 devices in a mesh: enc: 16 (over z, core), seq: 16 (over y, x).
Axes of the slice: x: 4, y: 4, z: 8, core: 2. Of those that a mesh axis runs over, the one named last changes fastest.
Arguments:
- queries: bfloat16 [16, 2048, 8192], P('enc', 'seq'), may hold values from -160 to 160
- kv_pool: bfloat16 [128, 2, 128, 8192], P('enc', None, None, 'seq'), may hold values from -16 to 16
- send_lists: int32 [16, 16, 1], P('enc'), may hold values from 0 to 7, as said below
- block_slots: int32 [16, 32, 2], P('enc'), may hold values from 0 to 15, as said below
- grad_context: bfloat16 [16, 2048, 8192], P('enc', 'seq'), may hold values from -24 to 24
Outputs:
- context: bfloat16 [16, 2048, 8192], P('enc', 'seq')
- grad_queries: bfloat16 [16, 2048, 8192], P('enc', 'seq')
- grad_pool: bfloat16 [128, 2, 128, 8192], P('enc', None, None, 'seq')
Inputs may be any that keep to these rules, and one draw needn't show every extreme that they name: send_lists[o, e] names 1 different local entries; each of a shard's 8 entries is named for at least one sequence. `block_slots`: the two slots of a block differ; every slot of a sequence is named by at least one of its blocks.
All inputs are finite; a program needn't handle non-finite values.
Results may differ from a plain program's by a relative error of at most 0.0065.
Values may be sent and summed in bfloat16 or wider, within the bound.
A program may use at most 128 MiB of HBM per device.

v0:
```python
import jax
import jax.numpy as jnp
from jax import lax
from jax.sharding import PartitionSpec as P

DH = 128
BLOCK = 64
NBLEN = 128


def to_heads(token_major):
    return lax.all_to_all(token_major, "seq", split_axis=2, concat_axis=1, tiled=True)


def to_tokens(head_major):
    return lax.all_to_all(head_major, "seq", split_axis=1, concat_axis=2, tiled=True)


def fetch_slots(kv_pool, entries):
    outgoing = kv_pool[entries]
    arrived = lax.all_to_all(outgoing, "enc", split_axis=0, concat_axis=0, tiled=True)
    return arrived.reshape((-1,) + kv_pool.shape[1:])


def move_up(row_data):
    filler = jnp.zeros((BLOCK - 1, row_data.shape[1]), row_data.dtype)
    return jnp.concatenate([row_data[BLOCK - 1 :], filler], axis=0)


def move_down(row_data):
    filler = jnp.zeros((BLOCK - 1, row_data.shape[1]), row_data.dtype)
    return jnp.concatenate([filler, row_data[: row_data.shape[0] - BLOCK + 1]], axis=0)


def into_blocks(head_rows, heads_here):
    blocks = head_rows.shape[0] // BLOCK
    return move_up(head_rows).reshape(blocks, BLOCK, heads_here, DH).transpose(0, 2, 1, 3)


def out_of_blocks(block_rows):
    blocks, heads_here = (block_rows.shape[0], block_rows.shape[1])
    return move_down(block_rows.transpose(0, 2, 1, 3).reshape(blocks * BLOCK, heads_here * DH))


def forward_parts(head_rows, arrived, block_use):
    slots = arrived.shape[0]
    heads_here = arrived.shape[-1] // DH
    queries_moved = into_blocks(head_rows, heads_here)
    pool_heads = arrived.reshape(slots, 2, NBLEN, heads_here, DH).transpose(0, 1, 3, 2, 4)
    keys_used = [pool_heads[:, 0][block_use[:, 0]], pool_heads[:, 0][block_use[:, 1]]]
    values_used = [pool_heads[:, 1][block_use[:, 0]], pool_heads[:, 1][block_use[:, 1]]]
    scores = [
        jnp.einsum("chid,chjd->chij", queries_moved, keys, preferred_element_type=jnp.float32)
        * DH ** (-0.5)
        for keys in keys_used
    ]
    row_peak = jnp.maximum(
        jnp.max(scores[0], axis=-1, keepdims=True), jnp.max(scores[1], axis=-1, keepdims=True)
    )
    weights = [jnp.exp(part_scores - row_peak) for part_scores in scores]
    total = jnp.sum(weights[0], axis=-1, keepdims=True) + jnp.sum(
        weights[1], axis=-1, keepdims=True
    )
    row_probs = [part_weights / total for part_weights in weights]
    probs_low = [part_probs.astype(jnp.bfloat16) for part_probs in row_probs]
    return (queries_moved, keys_used, values_used, row_probs, probs_low)


def local(queries, kv_pool, send_lists, block_slots, grad_context):
    block_use = block_slots[0]
    entries = send_lists[0]
    head_width = kv_pool.shape[-1]
    heads_here = head_width // DH
    score_scale = DH ** (-0.5)
    arrived = fetch_slots(kv_pool, entries)
    slots = arrived.shape[0]
    queries_moved, keys_used, values_used, row_probs, probs_low = forward_parts(
        to_heads(queries)[0], arrived, block_use
    )
    out_blocks = jnp.einsum(
        "chij,chjd->chid", probs_low[0], values_used[0], preferred_element_type=jnp.float32
    )
    out_blocks = out_blocks + jnp.einsum(
        "chij,chjd->chid", probs_low[1], values_used[1], preferred_element_type=jnp.float32
    )
    context = to_tokens(out_of_blocks(out_blocks.astype(jnp.bfloat16))[None])
    head_grads = to_heads(grad_context)[0]
    grads_moved = into_blocks(head_grads, heads_here)
    grad_probs = [
        jnp.einsum("chid,chjd->chij", grads_moved, values, preferred_element_type=jnp.float32)
        for values in values_used
    ]
    row_inner = jnp.sum(row_probs[0] * grad_probs[0], axis=-1, keepdims=True) + jnp.sum(
        row_probs[1] * grad_probs[1], axis=-1, keepdims=True
    )
    grad_scores = [
        (row_probs[n] * (grad_probs[n] - row_inner) * score_scale).astype(jnp.bfloat16)
        for n in range(2)
    ]
    query_grads = jnp.einsum(
        "chij,chjd->chid", grad_scores[0], keys_used[0], preferred_element_type=jnp.float32
    )
    query_grads = query_grads + jnp.einsum(
        "chij,chjd->chid", grad_scores[1], keys_used[1], preferred_element_type=jnp.float32
    )
    grad_queries = to_tokens(out_of_blocks(query_grads.astype(jnp.bfloat16))[None])
    slot_range = jnp.arange(slots, dtype=jnp.int32)
    slot_key = jnp.zeros((slots, heads_here, NBLEN, DH), jnp.float32)
    slot_value = jnp.zeros((slots, heads_here, NBLEN, DH), jnp.float32)
    for n in range(2):
        picker = (block_use[:, n][:, None] == slot_range[None, :]).astype(jnp.bfloat16)
        key_part = jnp.einsum(
            "chij,chid->chjd", grad_scores[n], queries_moved, preferred_element_type=jnp.float32
        ).astype(jnp.bfloat16)
        value_part = jnp.einsum(
            "chij,chid->chjd", probs_low[n], grads_moved, preferred_element_type=jnp.float32
        ).astype(jnp.bfloat16)
        slot_key = slot_key + jnp.einsum(
            "cs,chjd->shjd", picker, key_part, preferred_element_type=jnp.float32
        )
        slot_value = slot_value + jnp.einsum(
            "cs,chjd->shjd", picker, value_part, preferred_element_type=jnp.float32
        )
    slot_grads = jnp.stack([slot_key.astype(jnp.bfloat16), slot_value.astype(jnp.bfloat16)], axis=1)
    slot_grads = slot_grads.transpose(0, 1, 3, 2, 4).reshape(slots, 2, NBLEN, head_width)
    returned = lax.all_to_all(
        slot_grads.reshape(entries.shape + slot_grads.shape[1:]),
        "enc",
        split_axis=0,
        concat_axis=0,
        tiled=True,
    )
    returned = returned.reshape((-1,) + kv_pool.shape[1:])
    owner_pick = (
        entries.reshape(-1)[:, None] == jnp.arange(kv_pool.shape[0], dtype=jnp.int32)[None, :]
    ).astype(jnp.bfloat16)
    pool_grads = jnp.einsum(
        "ep,ekjw->pkjw", owner_pick, returned, preferred_element_type=jnp.float32
    )
    return (context, grad_queries, pool_grads.astype(jnp.bfloat16))


def solution(mesh):
    in_specs = (
        P("enc", "seq", None),
        P("enc", None, None, "seq"),
        P("enc", None, None),
        P("enc", None, None),
        P("enc", "seq", None),
    )
    out_specs = (P("enc", "seq", None), P("enc", "seq", None), P("enc", None, None, "seq"))
    return jax.shard_map(local, mesh=mesh, in_specs=in_specs, out_specs=out_specs, check_vma=False)
```

profile of v0, /device:TPU:1, one launch (start us, length us, event | category | flops | bytes accessed | tf_op | source)
XLA Modules:
  0.0 602.9 jit_solution(16944894643721143449)
XLA Ops:
  0.6 9.6 %copy.57 = bf16[1,128,8192]{1,0,2:T(2,128)(2,1)} copy(bf16[1,128,8192]{2,1,0:T(8,128)(2,1)} %param.5) | data formatting | bytes 4194304 | tf_op args[0]
  10.8 46.5 %reduce = bf16[8192,128]{1,0:T(8,128)(2,1)} reduce(bf16[8192,1,128]{2,1,0:T(2,128)(2,1)} %bitcast.134, bf16[]{:T(256)} %broadcast.101), dimensions={1}, to_apply=%bitcast.102.reduce_sub_computation | reduce | bytes 4194306
  61.2 7.6 %all-to-all-start = ((bf16[16,2,32768]{2,1,0:T(2,128)(2,1)}), bf16[16,2,32768]{2,1,0:T(2,128)(2,1)}, u32[]{:S(2)}, u32[]{:S(2)}) async-start(bf16[16,2,32768]{2,1,0:T(2,128)(2,1)} %reshape.129), calls=%async_computation | async-start | bytes 4194304 | tf_op jit(solution)/shard_map/all_to_all | solution.py:12
  68.9 9.5 %copy.66 = bf16[1,128,8192]{1,0,2:T(2,128)(2,1)} copy(bf16[1,128,8192]{2,1,0:T(8,128)(2,1)} %param.9) | data formatting | bytes 4194304 | tf_op args[4]
  78.3 46.5 %reduce.2 = bf16[8192,128]{1,0:T(8,128)(2,1)} reduce(bf16[8192,1,128]{2,1,0:T(2,128)(2,1)} %bitcast.141, bf16[]{:T(256)} %broadcast.101), dimensions={1}, to_apply=%bitcast.106.reduce_sub_computation | reduce | bytes 4194306
  128.8 6.7 %all-to-all-start.3 = ((bf16[16,2,32768]{2,1,0:T(2,128)(2,1)}), bf16[16,2,32768]{2,1,0:T(2,128)(2,1)}, u32[]{:S(2)}, u32[]{:S(2)}) async-start(bf16[16,2,32768]{2,1,0:T(2,128)(2,1)} %reshape.133), calls=%async_computation.3 | async-start | bytes 4194304 | tf_op jit(solution)/shard_map/all_to_all | solution.py:12
  138.3 26.0 %all-to-all-done.3 = bf16[16,2,32768]{2,1,0:T(2,128)(2,1)} async-done(((bf16[16,2,32768]{2,1,0:T(2,128)(2,1)}), bf16[16,2,32768]{2,1,0:T(2,128)(2,1)}, u32[]{:S(2)}, u32[]{:S(2)}) %all-to-all-start.3) | async-done | bytes 2097184 | tf_op jit(solution)/shard_map/all_to_all | solution.py:12
  164.2 11.7 %all-to-all-start.1 = ((bf16[16,1,2,128,512]{4,3,2,1,0:T(8,128)(2,1)}), bf16[16,1,2,128,512]{4,3,2,1,0:T(8,128)(2,1)}, u32[]{:S(2)}, u32[]{:S(2)}) async-start(bf16[16,1,2,128,512]{4,3,2,1,0:T(8,128)(2,1)} %bitcast.142), calls=%async_computation.1 | async-start | bytes 8388608 | tf_op jit(solution)/shard_map/all_to_all | solution.py:21
  175.9 10.5 %reshape.130 = bf16[8192,1,128]{2,1,0:T(2,128)(2,1)} reshape(bf16[16,2,32768]{2,1,0:T(2,128)(2,1)} %all-to-all-done) | data formatting | bytes 4194304
  197.5 10.5 %reshape.134 = bf16[8192,1,128]{2,1,0:T(2,128)(2,1)} reshape(bf16[16,2,32768]{2,1,0:T(2,128)(2,1)} %all-to-all-done.3) | data formatting | bytes 4194304
  223.1 46.4 %all-to-all-done.1 = bf16[16,1,2,128,512]{4,3,2,1,0:T(8,128)(2,1)} async-done(((bf16[16,1,2,128,512]{4,3,2,1,0:T(8,128)(2,1)}), bf16[16,1,2,128,512]{4,3,2,1,0:T(8,128)(2,1)}, u32[]{:S(2)}, u32[]{:S(2)}) %all-to-all-start.1) | async-done | bytes 4194336 | tf_op jit(solution)/shard_map/all_to_all | solution.py:21
  269.5 6.4 %copy.61 = bf16[16,1,2,128,512]{3,4,2,0,1:T(8,128)(2,1)} copy(bf16[16,1,2,128,512]{4,3,2,1,0:T(8,128)(2,1)} %all-to-all-done.1) | data formatting | bytes 8388608 | tf_op jit(solution)/shard_map/all_to_all | solution.py:21
  275.9 6.2 %copy.62 = bf16[16,2,128,4,128]{4,2,3,0,1:T(8,128)(2,1)} copy(bf16[16,2,128,4,128]{2,4,3,1,0:T(8,128)(2,1)} %bitcast.144) | data formatting | bytes 8388608 | tf_op jit(solution)/shard_map/reshape;reshape | solution.py:49
  282.1 4.8 slice_bitcast_fusion.1
  305.4 5.4 multiply_reduce_fusion.3
  327.9 18.5 %copy.158 = bf16[1,2048,512]{2,0,1:T(2,128)(2,1)} copy(bf16[1,2048,512]{2,1,0:T(8,128)(2,1)S(1)} %pad_bitcast_fusion.1) | data formatting | bytes 4194304 | tf_op jit(solution)/shard_map/broadcast_in_dim | solution.py:86
  346.4 15.4 %reduce.1 = bf16[2048,512]{1,0:T(8,128)(2,1)} reduce(bf16[2048,1,512]{2,1,0:T(2,128)(2,1)} %bitcast.138, bf16[]{:T(256)} %broadcast.101), dimensions={1}, to_apply=%bitcast.133.reduce_sub_computation | reduce | bytes 4194306
  370.9 5.9 fusion.23
  376.9 8.0 %multiply_reduce_fusion = (f32[32,4,64]{2,1,0:T(4,128)S(1)}, f32[32,4,64]{2,1,0:T(4,128)S(1)}, f32[32,4,64,128]{3,2,1,0:T(8,128)}) fusion(f32[32,4,64]{2,1,0:T(4,128)S(1)} %add.65, f32[32,4,64]{2,1,0:T(4,128)S(1)} %max.8, f32[32,4,64,128]{3,2,1,0:T(8,128)S(1)} %copy-done.5, f32[32,4,64,128]{3,2,1,0:T(8,128)S(1)} %fusion.23, ...), kind=kOutput, calls=%fused_computation.22 | convolution fusion | flops 278904832 | bytes 23199744 | tf_op jit(solution)/shard_map/chid,chjd->chij/dot_general | solution.py:90
  385.0 5.4 multiply_convert_fusion
  399.1 18.9 %copy.157 = bf16[1,2048,512]{2,0,1:T(2,128)(2,1)} copy(bf16[1,2048,512]{2,1,0:T(8,128)(2,1)S(1)} %pad_bitcast_fusion) | data formatting | bytes 4194304 | tf_op jit(solution)/shard_map/broadcast_in_dim | solution.py:106
  418.1 15.4 %reduce.3 = bf16[2048,512]{1,0:T(8,128)(2,1)} reduce(bf16[2048,1,512]{2,1,0:T(2,128)(2,1)} %bitcast.135, bf16[]{:T(256)} %broadcast.101), dimensions={1}, to_apply=%bitcast.132.reduce_sub_computation | reduce | bytes 4194306
  437.9 5.0 convolution_convert_fusion.3
  443.0 5.6 convolution_convert_fusion
  457.3 7.1 %all-to-all-start.4 = ((bf16[16,2,32768]{2,1,0:T(2,128)(2,1)}), bf16[16,2,32768]{2,1,0:T(2,128)(2,1)}, u32[]{:S(2)}, u32[]{:S(2)}) async-start(bf16[16,2,32768]{2,1,0:T(2,128)(2,1)} %reshape.135), calls=%async_computation.4 | async-start | bytes 4194304 | tf_op jit(solution)/shard_map/all_to_all | solution.py:16
  464.4 6.8 %convolution_convert_fusion.1 = bf16[32,4,128,128]{3,2,1,0:T(8,128)(2,1)S(1)} fusion(bf16[32,64,4,128]{3,2,1,0:T(4,128)(2,1)S(1)} %copy-done.18, f32[32,4,64,128]{3,2,1,0:T(8,128)} %copy-done.2, f32[32,4,64]{2,1,0:T(4,128)S(1)} %add.65, f32[32,4,64]{2,1,0:T(4,128)S(1)} %max.8), kind=kOutput, calls=%fused_computation.34 | convolution fusion | flops 274726912 | bytes 10551296 | tf_op jit(solution)/shard_map/chij,chid->chjd/dot_general | solution.py:115
  479.6 7.5 %copy.76 = bf16[16,2,128,4,128]{2,4,3,1,0:T(8,128)(2,1)} copy(bf16[16,2,128,4,128]{4,0,2,3,1:T(8,128)(2,1)} %maximum_bitcast_fusion) | data formatting | bytes 8388608 | tf_op jit(solution)/shard_map/transpose | solution.py:125
  487.1 6.4 %copy.77 = bf16[16,1,2,128,512]{4,3,2,1,0:T(8,128)(2,1)} copy(bf16[16,1,2,128,512]{3,4,2,0,1:T(8,128)(2,1)} %bitcast.145) | data formatting | bytes 8388608 | tf_op jit(solution)/shard_map/reshape;reshape | solution.py:127
  493.5 8.9 %all-to-all-start.5 = ((bf16[16,1,2,128,512]{4,3,2,1,0:T(8,128)(2,1)}), bf16[16,1,2,128,512]{4,3,2,1,0:T(8,128)(2,1)}, u32[]{:S(2)}, u32[]{:S(2)}) async-start(bf16[16,1,2,128,512]{4,3,2,1,0:T(8,128)(2,1)} %copy.77), calls=%async_computation.5 | async-start | bytes 8388608 | tf_op jit(solution)/shard_map/all_to_all | solution.py:126
  502.4 10.5 %reshape.132 = bf16[2048,1,512]{2,1,0:T(2,128)(2,1)} reshape(bf16[16,2,32768]{2,1,0:T(2,128)(2,1)} %all-to-all-done.2) | data formatting | bytes 4194304
  522.1 10.5 %reshape.136 = bf16[2048,1,512]{2,1,0:T(2,128)(2,1)} reshape(bf16[16,2,32768]{2,1,0:T(2,128)(2,1)} %all-to-all-done.4) | data formatting | bytes 4194304
  541.8 54.0 %all-to-all-done.5 = bf16[16,1,2,128,512]{4,3,2,1,0:T(8,128)(2,1)} async-done(((bf16[16,1,2,128,512]{4,3,2,1,0:T(8,128)(2,1)}), bf16[16,1,2,128,512]{4,3,2,1,0:T(8,128)(2,1)}, u32[]{:S(2)}, u32[]{:S(2)}) %all-to-all-start.5) | async-done | bytes 4194336 | tf_op jit(solution)/shard_map/all_to_all | solution.py:126
  (105 shorter events, 137.8 us)
Async XLA Ops:
  0.6 134.8 %copy-start = (bf16[8,2,128,512]{3,2,1,0:T(8,128)(2,1)S(1)}, bf16[8,2,128,512]{3,2,1,0:T(8,128)(2,1)}, u32[]{:S(2)}) copy-start(bf16[8,2,128,512]{3,2,1,0:T(8,128)(2,1)} %param.6) | copy-start | bytes 6291460
  61.2 67.5 %all-to-all-start = ((bf16[16,2,32768]{2,1,0:T(2,128)(2,1)}), bf16[16,2,32768]{2,1,0:T(2,128)(2,1)}, u32[]{:S(2)}, u32[]{:S(2)}) async-start(bf16[16,2,32768]{2,1,0:T(2,128)(2,1)} %reshape.129), calls=%async_computation | async-start | bytes 4194304 | tf_op jit(solution)/shard_map/all_to_all | solution.py:12
  124.8 10.6 %copy-start.21 = (s32[1,16,1]{1,2,0:T(1,128)S(1)}, s32[1,16,1]{1,2,0:T(1,128)}, u32[]{:S(2)}) copy-start(s32[1,16,1]{1,2,0:T(1,128)} %param.7) | copy-start | bytes 196
  128.8 35.5 %all-to-all-start.3 = ((bf16[16,2,32768]{2,1,0:T(2,128)(2,1)}), bf16[16,2,32768]{2,1,0:T(2,128)(2,1)}, u32[]{:S(2)}, u32[]{:S(2)}) async-start(bf16[16,2,32768]{2,1,0:T(2,128)(2,1)} %reshape.133), calls=%async_computation.3 | async-start | bytes 4194304 | tf_op jit(solution)/shard_map/all_to_all | solution.py:12
  164.2 11.7 %copy-start.20 = (s32[1,32,2]{1,2,0:T(2,128)S(1)}, s32[1,32,2]{1,2,0:T(2,128)}, u32[]{:S(2)}) copy-start(s32[1,32,2]{1,2,0:T(2,128)} %param.8) | copy-start | bytes 772
  164.2 105.3 %all-to-all-start.1 = ((bf16[16,1,2,128,512]{4,3,2,1,0:T(8,128)(2,1)}), bf16[16,1,2,128,512]{4,3,2,1,0:T(8,128)(2,1)}, u32[]{:S(2)}, u32[]{:S(2)}) async-start(bf16[16,1,2,128,512]{4,3,2,1,0:T(8,128)(2,1)} %bitcast.142), calls=%async_computation.1 | async-start | bytes 8388608 | tf_op jit(solution)/shard_map/all_to_all | solution.py:21
  305.4 5.4 copy-start.7
  310.8 7.0 %copy-start.2 = (f32[32,4,64,128]{3,2,1,0:T(8,128)}, f32[32,4,64,128]{3,2,1,0:T(8,128)S(1)}, u32[]{:S(2)}) copy-start(f32[32,4,64,128]{3,2,1,0:T(8,128)S(1)} %get-tuple-element.31) | copy-start | bytes 12582916
  314.0 7.8 %copy-start.4 = (f32[32,4,64,128]{3,2,1,0:T(8,128)}, f32[32,4,64,128]{3,2,1,0:T(8,128)S(1)}, u32[]{:S(2)}) copy-start(f32[32,4,64,128]{3,2,1,0:T(8,128)S(1)} %get-tuple-element.33) | copy-start | bytes 12582916
  314.0 3.9 copy-start.11
  317.9 4.0 copy-start.19
  366.2 91.1 %all-to-all-start.2 = ((bf16[16,2,32768]{2,1,0:T(2,128)(2,1)}), bf16[16,2,32768]{2,1,0:T(2,128)(2,1)}, u32[]{:S(2)}, u32[]{:S(2)}) async-start(bf16[16,2,32768]{2,1,0:T(2,128)(2,1)} %reshape.131), calls=%async_computation.2 | async-start | bytes 4194304 | tf_op jit(solution)/shard_map/all_to_all | solution.py:16
  370.9 6.0 copy-start.3
  370.9 6.0 copy-start.5
  370.9 6.0 copy-start.16
  385.0 5.4 copy-start.9
  390.3 1.3 copy-start.10
  391.6 3.3 copy-start.8
  437.9 5.0 copy-start.6
  437.9 5.0 copy-start.17
  448.5 4.4 copy-start.13
  457.3 7.1 %copy-start.18 = (bf16[32,64,4,128]{3,2,1,0:T(4,128)(2,1)S(1)}, bf16[32,64,4,128]{3,2,1,0:T(4,128)(2,1)}, u32[]{:S(2)}) copy-start(bf16[32,64,4,128]{3,2,1,0:T(4,128)(2,1)} %reshape.83) | copy-start | bytes 6291460
  457.3 36.2 %all-to-all-start.4 = ((bf16[16,2,32768]{2,1,0:T(2,128)(2,1)}), bf16[16,2,32768]{2,1,0:T(2,128)(2,1)}, u32[]{:S(2)}, u32[]{:S(2)}) async-start(bf16[16,2,32768]{2,1,0:T(2,128)(2,1)} %reshape.135), calls=%async_computation.4 | async-start | bytes 4194304 | tf_op jit(solution)/shard_map/all_to_all | solution.py:16
  464.4 6.8 %copy-start.15 = (f32[16,4,128,128]{3,0,2,1:T(8,128)S(1)}, f32[16,4,128,128]{3,0,2,1:T(8,128)}, u32[]{:S(2)}) copy-start(f32[16,4,128,128]{3,0,2,1:T(8,128)} %fusion.3) | copy-start | bytes 12582916
  471.2 2.6 copy-start.12
  471.2 3.5 copy-start.14
  493.5 102.3 %all-to-all-start.5 = ((bf16[16,1,2,128,512]{4,3,2,1,0:T(8,128)(2,1)}), bf16[16,1,2,128,512]{4,3,2,1,0:T(8,128)(2,1)}, u32[]{:S(2)}, u32[]{:S(2)}) async-start(bf16[16,1,2,128,512]{4,3,2,1,0:T(8,128)(2,1)} %copy.77), calls=%async_computation.5 | async-start | bytes 8388608 | tf_op jit(solution)/shard_map/all_to_all | solution.py:126
  535.4 60.5 %copy-start.22 = (s32[1,16,1]{1,2,0:T(1,128)S(1)}, s32[1,16,1]{1,2,0:T(1,128)}, u32[]{:S(2)}) copy-start(s32[1,16,1]{1,2,0:T(1,128)} %param.7) | copy-start | bytes 196
  595.9 6.8 %copy-start.1 = (bf16[8,2,128,512]{3,2,1,0:T(8,128)(2,1)S(1)}, bf16[8,2,128,512]{3,2,1,0:T(8,128)(2,1)}, u32[]{:S(2)}) copy-start(bf16[8,2,128,512]{3,2,1,0:T(8,128)(2,1)} %param.6) | copy-start | bytes 6291460
where the time goes:
time: 615 us; the launch traced here: 603 us
  local copies, waits for them, and re-layouts  222 us (36%)
  other arithmetic  135 us (22%)
  waiting for transfers between devices  126 us (20%)
  matrix products  71.4 us (12%)
  starting transfers between devices  46.5 us (8%)
    unnamed x4, other arithmetic  124 us
    unnamed x66, local copies, waits for them, and re-layouts  102 us
    all_to_all x1, waiting for transfers between devices, local(): lax.all_to_all(slot_grads.reshape(entries.shape + slot_grads.shape[1:]),...  54 us
    all_to_all x1, waiting for transfers between devices, fetch_slots(): lax.all_to_all(outgoing, 'enc', split_axis=0, concat_axis=0, tiled=True)  46.4 us
    all_to_all x2, waiting for transfers between devices, to_heads(): lax.all_to_all(token_major, 'seq', split_axis=2, concat_axis=1, tiled=True)  26 us
    broadcast_in_dim x2, local copies, waits for them, and re-layouts, local(): out_of_blocks(query_grads.astype(jnp.bfloat16))[None]  19.4 us
    broadcast_in_dim x2, local copies, waits for them, and re-layouts, local(): context = to_tokens(out_of_blocks(out_blocks.astype(jnp.bfloat16))[None])  19 us
    all_to_all x2, starting transfers between devices, to_heads(): lax.all_to_all(token_major, 'seq', split_axis=2, concat_axis=1, tiled=True)  14.3 us
  transfers between devices with their start and end apart: 6, of which 3 were waited for; matrix products, arithmetic and copies ran while one was open for 44% of the time, Pallas kernels for 0%

commit v1 on v0

--- a/solution.py
+++ b/solution.py
@@ -1,11 +1,22 @@
+import functools
 import jax
 import jax.numpy as jnp
 from jax import lax
 from jax.sharding import PartitionSpec as P
+from jax.lax import all_to_all, axis_size
 
 DH = 128
 BLOCK = 64
 NBLEN = 128
+
+
+def _unite_boxes(my_data, array_dim, along_dim):
+    t_next = jnp.split(my_data, axis_size("seq"), array_dim)
+    tile_out = all_to_all(jnp.stack(t_next, 0), axis_name="seq", split_axis=0, concat_axis=0)
+    return jnp.concatenate(tile_out, along_dim)
+
+
+press_sites = functools.partial(_unite_boxes, array_dim=1, along_dim=2)
 
 
 def to_heads(token_major):
@@ -13,7 +24,7 @@
 
 
 def to_tokens(head_major):
-    return lax.all_to_all(head_major, "seq", split_axis=1, concat_axis=2, tiled=True)
+    return press_sites(head_major)
 
 
 def fetch_slots(kv_pool, entries):

time: 615 us -> 561 us (0.912)
  local copies, waits for them, and re-layouts: 222 us -> 171 us
  other arithmetic: 135 us -> 105 us
  waiting for transfers between devices: 126 us -> 154 us
    unnamed x4 -> x2, other arithmetic: 124 us -> 93 us
    all_to_all x1, waiting for transfers between devices: 54 us -> 81.6 us  [local(): lax.all_to_all(slot_grads.reshape(entries.shape + slot_grads.shape[1:]),...]
    broadcast_in_dim x2 -> x1, local copies, waits for them, and re-layouts: 19.4 us -> 0.49 us  [local(): out_of_blocks(query_grads.astype(jnp.bfloat16))[None]]
    broadcast_in_dim x2 -> x1, local copies, waits for them, and re-layouts: 19 us -> 0.49 us  [local(): context = to_tokens(out_of_blocks(out_blocks.astype(jnp.bfloat16))[None])]
    unnamed x66 -> x82, local copies, waits for them, and re-layouts: 102 us -> 85.9 us
  transfers between devices with their start and end apart: 6 -> 6, of which waited for: 3 -> 3; matrix products, arithmetic and copies ran while one was open for 44% -> 34% of each run, Pallas kernels for 0% -> 0%
where the time goes in v1:
time: 561 us; the launch traced here: 550 us
  local copies, waits for them, and re-layouts  171 us (30%)
  waiting for transfers between devices  154 us (27%)
  other arithmetic  105 us (19%)
  matrix products  71.5 us (13%)
  starting transfers between devices  46.6 us (8%)
    unnamed x2, other arithmetic  93 us
    unnamed x82, local copies, waits for them, and re-layouts  85.9 us
    all_to_all x1, waiting for transfers between devices, local(): lax.all_to_all(slot_grads.reshape(entries.shape + slot_grads.shape[1:]),...  81.6 us
    all_to_all x1, waiting for transfers between devices, fetch_slots(): lax.all_to_all(outgoing, 'enc', split_axis=0, concat_axis=0, tiled=True)  46.4 us
    all_to_all x2, waiting for transfers between devices, to_heads(): lax.all_to_all(token_major, 'seq', split_axis=2, concat_axis=1, tiled=True)  26 us
    all_to_all x2, starting transfers between devices, to_heads(): lax.all_to_all(token_major, 'seq', split_axis=2, concat_axis=1, tiled=True)  14.4 us
    dot_general x2, matrix products, local(): jnp.einsum('chij,chid->chjd', probs_low[n], grads_moved, preferred_elemen...  12.3 us
    all_to_all x1, starting transfers between devices, fetch_slots(): lax.all_to_all(outgoing, 'enc', split_axis=0, concat_axis=0, tiled=True)  11.7 us
  transfers between devices with their start and end apart: 6, of which 3 were waited for; matrix products, arithmetic and copies ran while one was open for 34% of the time, Pallas kernels for 0%

profile of v1, /device:TPU:1, one launch (start us, length us, event | category | flops | bytes accessed | tf_op | source)
XLA Modules:
  0.0 550.1 jit_solution(11700869312573791062)
XLA Ops:
  0.6 9.6 %copy.87 = bf16[1,128,8192]{1,0,2:T(2,128)(2,1)} copy(bf16[1,128,8192]{2,1,0:T(8,128)(2,1)} %param.5) | data formatting | bytes 4194304 | tf_op args[0]
  10.8 46.5 %reduce = bf16[8192,128]{1,0:T(8,128)(2,1)} reduce(bf16[8192,1,128]{2,1,0:T(2,128)(2,1)} %bitcast.250, bf16[]{:T(256)} %broadcast.101), dimensions={1}, to_apply=%bitcast.226.reduce_sub_computation | reduce | bytes 4194306
  61.2 7.6 %all-to-all-start = ((bf16[16,2,32768]{2,1,0:T(2,128)(2,1)}), bf16[16,2,32768]{2,1,0:T(2,128)(2,1)}, u32[]{:S(2)}, u32[]{:S(2)}) async-start(bf16[16,2,32768]{2,1,0:T(2,128)(2,1)} %reshape.145), calls=%async_computation | async-start | bytes 4194304 | tf_op jit(solution)/shard_map/all_to_all | solution.py:23
  68.9 9.5 %copy.95 = bf16[1,128,8192]{1,0,2:T(2,128)(2,1)} copy(bf16[1,128,8192]{2,1,0:T(8,128)(2,1)} %param.9) | data formatting | bytes 4194304 | tf_op args[4]
  78.3 46.5 %reduce.1 = bf16[8192,128]{1,0:T(8,128)(2,1)} reduce(bf16[8192,1,128]{2,1,0:T(2,128)(2,1)} %bitcast.251, bf16[]{:T(256)} %broadcast.101), dimensions={1}, to_apply=%bitcast.228.reduce_sub_computation | reduce | bytes 4194306
  128.8 6.8 %all-to-all-start.3 = ((bf16[16,2,32768]{2,1,0:T(2,128)(2,1)}), bf16[16,2,32768]{2,1,0:T(2,128)(2,1)}, u32[]{:S(2)}, u32[]{:S(2)}) async-start(bf16[16,2,32768]{2,1,0:T(2,128)(2,1)} %reshape.147), calls=%async_computation.3 | async-start | bytes 4194304 | tf_op jit(solution)/shard_map/all_to_all | solution.py:23
  138.4 26.0 %all-to-all-done.3 = bf16[16,2,32768]{2,1,0:T(2,128)(2,1)} async-done(((bf16[16,2,32768]{2,1,0:T(2,128)(2,1)}), bf16[16,2,32768]{2,1,0:T(2,128)(2,1)}, u32[]{:S(2)}, u32[]{:S(2)}) %all-to-all-start.3) | async-done | bytes 2097184 | tf_op jit(solution)/shard_map/all_to_all | solution.py:23
  164.4 11.7 %all-to-all-start.1 = ((bf16[16,1,2,128,512]{4,3,2,1,0:T(8,128)(2,1)}), bf16[16,1,2,128,512]{4,3,2,1,0:T(8,128)(2,1)}, u32[]{:S(2)}, u32[]{:S(2)}) async-start(bf16[16,1,2,128,512]{4,3,2,1,0:T(8,128)(2,1)} %bitcast.254), calls=%async_computation.1 | async-start | bytes 8388608 | tf_op jit(solution)/shard_map/all_to_all | solution.py:32
  176.1 10.4 %reshape.146 = bf16[8192,1,128]{2,1,0:T(2,128)(2,1)} reshape(bf16[16,2,32768]{2,1,0:T(2,128)(2,1)} %all-to-all-done) | data formatting | bytes 4194304
  197.7 10.4 %reshape.148 = bf16[8192,1,128]{2,1,0:T(2,128)(2,1)} reshape(bf16[16,2,32768]{2,1,0:T(2,128)(2,1)} %all-to-all-done.3) | data formatting | bytes 4194304
  223.3 46.4 %all-to-all-done.1 = bf16[16,1,2,128,512]{4,3,2,1,0:T(8,128)(2,1)} async-done(((bf16[16,1,2,128,512]{4,3,2,1,0:T(8,128)(2,1)}), bf16[16,1,2,128,512]{4,3,2,1,0:T(8,128)(2,1)}, u32[]{:S(2)}, u32[]{:S(2)}) %all-to-all-start.1) | async-done | bytes 4194336 | tf_op jit(solution)/shard_map/all_to_all | solution.py:32
  269.7 6.4 %copy.91 = bf16[16,1,2,128,512]{3,4,2,0,1:T(8,128)(2,1)} copy(bf16[16,1,2,128,512]{4,3,2,1,0:T(8,128)(2,1)} %all-to-all-done.1) | data formatting | bytes 8388608 | tf_op jit(solution)/shard_map/all_to_all | solution.py:32
  276.1 6.2 %copy.92 = bf16[16,2,128,4,128]{4,2,3,0,1:T(8,128)(2,1)} copy(bf16[16,2,128,4,128]{2,4,3,1,0:T(8,128)(2,1)} %bitcast.256) | data formatting | bytes 8388608 | tf_op jit(solution)/shard_map/reshape;reshape | solution.py:60
  282.3 4.8 slice_bitcast_fusion.1
  287.1 4.6 gather_fusion.3
  291.7 4.6 gather_fusion.1
  296.3 4.6 gather_fusion.2
  301.0 4.6 gather_fusion.4
  305.6 5.4 multiply_reduce_fusion.3
  318.1 4.7 fusion.53
  325.7 8.0 %multiply_reduce_fusion = (f32[32,4,64]{2,1,0:T(4,128)S(1)}, f32[32,4,64]{2,1,0:T(4,128)S(1)}, f32[32,4,64,128]{3,2,1,0:T(8,128)}) fusion(f32[32,4,64]{2,1,0:T(4,128)S(1)} %add.65, f32[32,4,64]{2,1,0:T(4,128)S(1)} %max.8, f32[32,4,64,128]{3,2,1,0:T(8,128)S(1)} %get-tuple-element.33, f32[32,4,64,128]{3,2,1,0:T(8,128)S(1)} %fusion.23, ...), kind=kOutput, calls=%fused_computation.22 | convolution fusion | flops 278904832 | bytes 23199744 | tf_op jit(solution)/shard_map/chid,chjd->chij/dot_general | solution.py:101
  333.8 6.2 %multiply_convert_fusion = (bf16[32,4,64,128]{3,2,1,0:T(8,128)(2,1)}, bf16[32,4,64,128]{3,2,1,0:T(8,128)(2,1)S(1)}) fusion(f32[32,4,64,128]{3,2,1,0:T(8,128)} %get-tuple-element.34, f32[32,4,64]{2,1,0:T(4,128)S(1)} %add.67, f32[32,4,64]{2,1,0:T(4,128)S(1)} %add.65, f32[32,4,64]{2,1,0:T(4,128)S(1)} %max.8, f32[32,4,64,128]{3,2,1,0:T(8,128)S(1)} %get-tuple-element.33, ...), kind=kLoop, calls=%fused_computation.20 | loop fusion | flops 14680064 | bytes 21069824 | tf_op jit(solution)/shard_map/convert_element_type | solution.py:108
  364.8 4.6 all-to-all-start.2
  390.1 5.5 convolution_convert_fusion
  400.0 4.4 fusion.7
  404.4 7.0 %all-to-all-start.4 = ((bf16[16,1,128,512]{3,2,1,0:T(8,128)(2,1)}), bf16[16,1,128,512]{3,2,1,0:T(8,128)(2,1)}, u32[]{:S(2)}, u32[]{:S(2)}) async-start(bf16[16,1,128,512]{3,2,1,0:T(8,128)(2,1)} %fusion.55), calls=%async_computation.4 | async-start | bytes 4194304 | tf_op jit(solution)/shard_map/all_to_all | solution.py:15
  411.4 6.8 %convolution_convert_fusion.1 = bf16[32,4,128,128]{3,2,1,0:T(8,128)(2,1)S(1)} fusion(bf16[32,64,4,128]{3,2,1,0:T(4,128)(2,1)S(1)} %copy-done.14, f32[32,4,64,128]{3,2,1,0:T(8,128)} %copy-done.2, f32[32,4,64]{2,1,0:T(4,128)S(1)} %add.65, f32[32,4,64]{2,1,0:T(4,128)S(1)} %max.8), kind=kOutput, calls=%fused_computation.34 | convolution fusion | flops 274726912 | bytes 10551296 | tf_op jit(solution)/shard_map/chij,chid->chjd/dot_general | solution.py:126
  426.6 7.5 %copy.104 = bf16[16,2,128,4,128]{2,4,3,1,0:T(8,128)(2,1)} copy(bf16[16,2,128,4,128]{4,0,2,3,1:T(8,128)(2,1)} %maximum_bitcast_fusion) | data formatting | bytes 8388608 | tf_op jit(solution)/shard_map/transpose | solution.py:136
  434.1 6.4 %copy.105 = bf16[16,1,2,128,512]{4,3,2,1,0:T(8,128)(2,1)} copy(bf16[16,1,2,128,512]{3,4,2,0,1:T(8,128)(2,1)} %bitcast.257) | data formatting | bytes 8388608 | tf_op jit(solution)/shard_map/reshape;reshape | solution.py:138
  440.5 8.9 %all-to-all-start.5 = ((bf16[16,1,2,128,512]{4,3,2,1,0:T(8,128)(2,1)}), bf16[16,1,2,128,512]{4,3,2,1,0:T(8,128)(2,1)}, u32[]{:S(2)}, u32[]{:S(2)}) async-start(bf16[16,1,2,128,512]{4,3,2,1,0:T(8,128)(2,1)} %copy.105), calls=%async_computation.5 | async-start | bytes 8388608 | tf_op jit(solution)/shard_map/all_to_all | solution.py:137
  461.3 81.6 %all-to-all-done.5 = bf16[16,1,2,128,512]{4,3,2,1,0:T(8,128)(2,1)} async-done(((bf16[16,1,2,128,512]{4,3,2,1,0:T(8,128)(2,1)}), bf16[16,1,2,128,512]{4,3,2,1,0:T(8,128)(2,1)}, u32[]{:S(2)}, u32[]{:S(2)}) %all-to-all-start.5) | async-done | bytes 4194336 | tf_op jit(solution)/shard_map/all_to_all | solution.py:137
  542.8 4.7 fusion.31
  (119 shorter events, 119.4 us)
Async XLA Ops:
  0.6 135.0 %copy-start = (bf16[8,2,128,512]{3,2,1,0:T(8,128)(2,1)S(1)}, bf16[8,2,128,512]{3,2,1,0:T(8,128)(2,1)}, u32[]{:S(2)}) copy-start(bf16[8,2,128,512]{3,2,1,0:T(8,128)(2,1)} %param.6) | copy-start | bytes 6291460
  61.2 67.6 %all-to-all-start = ((bf16[16,2,32768]{2,1,0:T(2,128)(2,1)}), bf16[16,2,32768]{2,1,0:T(2,128)(2,1)}, u32[]{:S(2)}, u32[]{:S(2)}) async-start(bf16[16,2,32768]{2,1,0:T(2,128)(2,1)} %reshape.145), calls=%async_computation | async-start | bytes 4194304 | tf_op jit(solution)/shard_map/all_to_all | solution.py:23
  128.8 6.8 %copy-start.17 = (s32[1,16,1]{1,2,0:T(1,128)S(1)}, s32[1,16,1]{1,2,0:T(1,128)}, u32[]{:S(2)}) copy-start(s32[1,16,1]{1,2,0:T(1,128)} %param.7) | copy-start | bytes 196
  128.8 35.6 %all-to-all-start.3 = ((bf16[16,2,32768]{2,1,0:T(2,128)(2,1)}), bf16[16,2,32768]{2,1,0:T(2,128)(2,1)}, u32[]{:S(2)}, u32[]{:S(2)}) async-start(bf16[16,2,32768]{2,1,0:T(2,128)(2,1)} %reshape.147), calls=%async_computation.3 | async-start | bytes 4194304 | tf_op jit(solution)/shard_map/all_to_all | solution.py:23
  164.4 11.7 %copy-start.16 = (s32[1,32,2]{1,2,0:T(2,128)S(1)}, s32[1,32,2]{1,2,0:T(2,128)}, u32[]{:S(2)}) copy-start(s32[1,32,2]{1,2,0:T(2,128)} %param.8) | copy-start | bytes 772
  164.4 105.3 %all-to-all-start.1 = ((bf16[16,1,2,128,512]{4,3,2,1,0:T(8,128)(2,1)}), bf16[16,1,2,128,512]{4,3,2,1,0:T(8,128)(2,1)}, u32[]{:S(2)}, u32[]{:S(2)}) async-start(bf16[16,1,2,128,512]{4,3,2,1,0:T(8,128)(2,1)} %bitcast.254), calls=%async_computation.1 | async-start | bytes 8388608 | tf_op jit(solution)/shard_map/all_to_all | solution.py:32
  305.6 5.4 copy-start.5
  311.0 22.7 %copy-start.2 = (f32[32,4,64,128]{3,2,1,0:T(8,128)}, f32[32,4,64,128]{3,2,1,0:T(8,128)S(1)}, u32[]{:S(2)}) copy-start(f32[32,4,64,128]{3,2,1,0:T(8,128)S(1)} %get-tuple-element.31) | copy-start | bytes 12582916
  314.2 32.6 %copy-start.3 = (f32[32,4,64,128]{3,2,1,0:T(8,128)}, f32[32,4,64,128]{3,2,1,0:T(8,128)S(1)}, u32[]{:S(2)}) copy-start(f32[32,4,64,128]{3,2,1,0:T(8,128)S(1)} %get-tuple-element.33) | copy-start | bytes 12582916
  314.2 3.9 copy-start.10
  318.1 4.7 copy-start.13
  333.8 6.3 %copy-start.7 = (bf16[32,4,128,128]{3,2,1,0:T(8,128)(2,1)S(1)}, bf16[32,4,128,128]{3,2,1,0:T(8,128)(2,1)}, u32[]{:S(2)}) copy-start(bf16[32,4,128,128]{3,2,1,0:T(8,128)(2,1)} %gather_fusion.1) | copy-start | bytes 12582916
  343.2 3.5 copy-start.15
  343.2 5.0 copy-start.18
  364.8 39.6 %all-to-all-start.2 = ((bf16[16,1,128,512]{3,2,1,0:T(8,128)(2,1)}), bf16[16,1,128,512]{3,2,1,0:T(8,128)(2,1)}, u32[]{:S(2)}, u32[]{:S(2)}) async-start(bf16[16,1,128,512]{3,2,1,0:T(8,128)(2,1)} %fusion.71), calls=%async_computation.2 | async-start | bytes 4194304 | tf_op jit(solution)/shard_map/all_to_all | solution.py:15
  369.4 3.1 copy-start.6
  369.4 3.5 copy-start.8
  378.9 11.1 %copy-start.4 = (f32[32,4,64,128]{3,2,1,0:T(8,128)S(1)}, f32[32,4,64,128]{3,2,1,0:T(8,128)}, u32[]{:S(2)}) copy-start(f32[32,4,64,128]{3,2,1,0:T(8,128)} %copy-done.3) | copy-start | bytes 12582916
  379.4 10.6 %copy-start.14 = (bf16[32,64,4,128]{3,2,1,0:T(4,128)(2,1)S(1)}, bf16[32,64,4,128]{3,2,1,0:T(4,128)(2,1)}, u32[]{:S(2)}) copy-start(bf16[32,64,4,128]{3,2,1,0:T(4,128)(2,1)} %reshape.97) | copy-start | bytes 6291460
  404.4 36.1 %all-to-all-start.4 = ((bf16[16,1,128,512]{3,2,1,0:T(8,128)(2,1)}), bf16[16,1,128,512]{3,2,1,0:T(8,128)(2,1)}, u32[]{:S(2)}, u32[]{:S(2)}) async-start(bf16[16,1,128,512]{3,2,1,0:T(8,128)(2,1)} %fusion.55), calls=%async_computation.4 | async-start | bytes 4194304 | tf_op jit(solution)/shard_map/all_to_all | solution.py:15
  411.4 6.8 %copy-start.12 = (f32[16,4,128,128]{3,0,2,1:T(8,128)S(1)}, f32[16,4,128,128]{3,0,2,1:T(8,128)}, u32[]{:S(2)}) copy-start(f32[16,4,128,128]{3,0,2,1:T(8,128)} %fusion.3) | copy-start | bytes 12582916
  418.2 2.6 copy-start.9
  418.2 3.5 copy-start.11
  440.5 102.4 %all-to-all-start.5 = ((bf16[16,1,2,128,512]{4,3,2,1,0:T(8,128)(2,1)}), bf16[16,1,2,128,512]{4,3,2,1,0:T(8,128)(2,1)}, u32[]{:S(2)}, u32[]{:S(2)}) async-start(bf16[16,1,2,128,512]{4,3,2,1,0:T(8,128)(2,1)} %copy.105), calls=%async_computation.5 | async-start | bytes 8388608 | tf_op jit(solution)/shard_map/all_to_all | solution.py:137
  542.8 6.8 %copy-start.1 = (bf16[8,2,128,512]{3,2,1,0:T(8,128)(2,1)S(1)}, bf16[8,2,128,512]{3,2,1,0:T(8,128)(2,1)}, u32[]{:S(2)}) copy-start(bf16[8,2,128,512]{3,2,1,0:T(8,128)(2,1)} %param.6) | copy-start | bytes 6291460
